TPU v7x, 32 devices: a whole 2x2x4 slice. The times are simulated.
32 devices in a mesh: row: 4 (over z), col: 2 (over x), depth: 4 (over y, core).
Axes of the slice: x: 2, y: 2, z: 4, core: 2. Of those that a mesh axis runs over, the one named last changes fastest.
Arguments:
- amplitudes: bfloat16 [3200, 7200], P('row', ('col', 'depth')), may hold values from -6 to 6
- integrals: bfloat16 [7200, 4096], P('row', ('col', 'depth')), may hold values from -0.0625 to 0.0625
- cycle_integrals: bfloat16 [256, 256], P('row'), as said below
- occ_irrep: int32 [100], replicated, may hold values from 0 to 7
- vir_irrep: int32 [900], replicated, may hold values from 0 to 7
Outputs:
- ladder: bfloat16 [3200, 4096], P('row', ('col', 'depth'))
- cycle: bfloat16 [256, 57600], P('row', ('col', 'depth'))
Inputs may be any that keep to these rules, and one draw needn't show every extreme that they name: cycle_integrals equals its transpose.
All inputs are finite; a program needn't handle non-finite values.
Results may differ from a plain program's by a relative error of at most 0.001.
Values may be sent and summed in bfloat16 or wider, within the bound.
A program may use at most 128 MiB of HBM per device.

v0:
```python
import jax
import jax.numpy as jnp
from jax import lax
from jax.sharding import PartitionSpec as P

NO = 100
NV = 900
JW = 64
CW = 8


def label_bits(labels):
    return jnp.stack([labels % 2, labels // 2 % 2, labels // 4 % 2])


def lookup(lookup_table, indices):
    matches = indices[:, None] == jnp.arange(lookup_table.shape[0], dtype=jnp.int32)[None, :]
    return jnp.sum(jnp.where(matches, lookup_table[None, :], 0), axis=1)


def shards(amplitudes, integrals, cycle_integrals, occ_irrep, vir_irrep):
    rows_here = amplitudes.shape[0]
    occ_block = rows_here // NO
    local_cols = amplitudes.shape[1]
    regroup_in = amplitudes.reshape(occ_block, NO, local_cols)[:, :JW, :]
    spread = lax.all_to_all(regroup_in, ("col", "depth"), split_axis=1, concat_axis=2, tiled=True)
    occ_here = spread.shape[1]
    ordered = (
        spread.reshape(occ_block, occ_here, CW, NV)
        .transpose(0, 2, 1, 3)
        .reshape(occ_block * CW, occ_here * NV)
    )
    columns = occ_here * NV
    integ_all = lax.all_gather(integrals, "row", axis=0, tiled=True)
    ladder_sum = jnp.dot(
        lax.all_gather(amplitudes, ("col", "depth"), axis=1, tiled=True),
        integ_all,
        preferred_element_type=jnp.float32,
    )
    ladder = ladder_sum.astype(jnp.bfloat16)
    cycle_rows_here = cycle_integrals.shape[0]
    cycle_sum = lax.psum_scatter(
        lax.dot_general(
            cycle_integrals, ordered, (((0,), (0,)), ((), ())), preferred_element_type=jnp.float32
        ),
        "row",
        scatter_dimension=0,
        tiled=True,
    )
    occ_bits = label_bits(occ_irrep)
    vir_bits = label_bits(vir_irrep)
    row_ids = lax.axis_index("row") * cycle_rows_here + jnp.arange(cycle_rows_here, dtype=jnp.int32)
    column_ids = lax.axis_index(("col", "depth")) * columns + jnp.arange(columns, dtype=jnp.int32)
    occ_first = row_ids // CW
    virt_first = row_ids % CW
    occ_second = column_ids // NV
    virt_second = column_ids % NV
    odd_count = jnp.zeros((cycle_rows_here, columns), jnp.int32)
    for digit in range(3):
        row_bits = lookup(occ_bits[digit], occ_first) + lookup(vir_bits[digit], virt_first)
        column_bits = lookup(occ_bits[digit], occ_second) + lookup(vir_bits[digit], virt_second)
        odd_count = odd_count + (row_bits[:, None] + column_bits[None, :]) % 2
    cycle = jnp.where(odd_count == 0, cycle_sum, jnp.float32(0.0)).astype(jnp.bfloat16)
    return (ladder, cycle)


def solution(mesh):
    in_specs = (P("row", ("col", "depth")), P("row", ("col", "depth")), P("row", None), P(), P())
    out_specs = (P("row", ("col", "depth")), P("row", ("col", "depth")))
    return jax.shard_map(shards, mesh=mesh, in_specs=in_specs, out_specs=out_specs, check_vma=False)
```

profile of v0, /device:TPU:0, one launch (start us, length us, event | category | flops | bytes accessed | tf_op | source)
XLA Modules:
  0.0 310.4 jit_solution(11669424504243657550)
XLA Ops:
  8.0 0.0 copy-start
  8.0 0.0 reduce-scatter.2.cloned.1.call-start
  8.1 3.8 %reshape.104 = bf16[8,100,900]{1,0,2:T(8,128)(2,1)S(1)} reshape(bf16[800,900]{0,1:T(8,128)(2,1)} %param.5) | data formatting | bytes 2880000 | tf_op jit(solution)/shard_map/reshape | solution.py:25
  11.8 2.8 copy.15
  14.7 19.6 %all_to_all.4 = bf16[8,64,900]{2,0,1:T(8,128)(2,1)S(1)} all-to-all(bf16[8,64,900]{2,0,1:T(8,128)(2,1)S(1)} %copy.15), channel_id=1, replica_groups=mesh['row'=4,'col'=2,'depth'=4] {'col','depth'}, dimensions={1} | all-to-all | bytes 1843200 | tf_op jit(solution)/shard_map/all_to_all | solution.py:26
  34.3 0.6 copy.16
  34.9 1.3 reshape.100
  36.2 0.0 copy-done
  36.2 4.2 %fusion.18 = f32[256,7200]{1,0:T(8,128)} fusion(bf16[64,256]{1,0:T(8,128)(2,1)S(1)} %copy-done, bf16[64,7200]{1,0:T(8,128)(2,1)S(1)} %reshape.100), kind=kOutput, calls=%fused_computation.91 | convolution fusion | flops 235929600 | bytes 8327168 | tf_op jit(solution)/shard_map/dot_general | solution.py:43
  40.4 0.0 reduce-scatter.2.cloned.1.call-update
  40.4 0.0 copy-start.2
  40.4 0.0 copy-start.1
  40.5 0.0 all-gather.6.cloned.1.call-start
  40.5 0.5 all-gather.6.cloned.1.call-update
  41.0 0.2 all-gather.4.cloned.1.call-start
  41.3 0.4 all-gather.4.cloned.1.call-update
  41.7 0.0 copy-done.2
  41.7 0.0 copy-done.1
  41.7 1.1 select_reduce_fusion.5
  42.9 9.3 %select_reduce_fusion.2 = (s32[7200]{0:T(1024)S(1)}, s32[7200]{0:T(1024)S(1)}, s32[7200]{0:T(1024)S(1)}) fusion(s32[900]{0:T(1024)S(1)} %get-tuple-element.16, s32[7200]{0:T(1024)S(1)} %get-tuple-element.20, s32[900]{0:T(1024)S(1)} %get-tuple-element.15, s32[900]{0:T(1024)S(1)} %get-tuple-element.14), kind=kLoop, calls=%fused_computation.2 | loop fusion | flops 45338400 | bytes 126000 | tf_op jit(solution)/shard_map/reduce_sum | solution.py:18
  52.2 0.2 select_reduce_fusion.11
  52.4 0.3 select_reduce_fusion.8
  52.8 157.8 %reduce-scatter.2.cloned.1.call-done = f32[64,7200]{1,0:T(8,128)} async-done(((f32[256,7200]{1,0:T(8,128)}), f32[64,7200]{1,0:T(8,128)}) %reduce-scatter.2.cloned.1.call-update) | async-done | bytes 1843216 | tf_op jit(solution)/shard_map/reduce_scatter | solution.py:42
  210.5 4.6 %select_convert_fusion = bf16[64,7200]{1,0:T(8,128)(2,1)} fusion(f32[64,7200]{1,0:T(8,128)} %reduce-scatter.2.cloned.1.call-done, s32[7200]{0:T(1024)S(1)} %add.222, s32[64]{0:T(128)S(1)} %add.220, s32[7200]{0:T(1024)S(1)} %add.213, s32[64]{0:T(128)S(1)} %add.211, s32[7200]{0:T(1024)S(1)} %add.205, s32[64]{0:T(128)S(1)} %add.199), kind=kLoop, calls=%fused_computation.29 | loop fusion | flops 18432000 | bytes 2851968 | tf_op jit(solution)/shard_map/convert_element_type | solution.py:63
  215.1 0.0 all-gather.6.cloned.1.call-done
  215.1 12.2 %reshape.103 = bf16[7200,800]{1,0:T(8,128)(2,1)} reshape(bf16[8,900,800]{2,1,0:T(8,128)(2,1)} %all-gather.6.cloned.1.call-done) | data formatting | bytes 23040000
  227.3 61.8 %all-gather.4.cloned.1.call-done = bf16[7200,512]{1,0:T(8,128)(2,1)} async-done(((bf16[1800,512]{1,0:T(8,128)(2,1)}), bf16[7200,512]{1,0:T(8,128)(2,1)}) %all-gather.4.cloned.1.call-update) | async-done | bytes 7372816 | tf_op jit(solution)/shard_map/all_gather | solution.py:34
  289.1 13.9 %convolution_convert_fusion = bf16[800,512]{1,0:T(8,128)(2,1)} fusion(bf16[7200,800]{1,0:T(8,128)(2,1)} %reshape.103, bf16[7200,512]{1,0:T(8,128)(2,1)} %all-gather.4.cloned.1.call-done), kind=kOutput, calls=%fused_computation.30 | convolution fusion | flops 5898649600 | bytes 19712000 | tf_op jit(solution)/shard_map/dot_general | solution.py:35
  (10 shorter events, 0.1 us)
Async XLA Ops:
  8.0 28.2 %copy-start = (bf16[64,256]{1,0:T(8,128)(2,1)S(1)}, bf16[64,256]{1,0:T(8,128)(2,1)}, u32[]{:S(2)}) copy-start(bf16[64,256]{1,0:T(8,128)(2,1)} %param.7) | copy-start | bytes 98308
  8.0 202.5 %reduce-scatter.2.cloned.1.call-start = ((), (), s32[]{:S(2)}) async-start(), calls=%async_computation.3 | async-start | bytes 9338880 | tf_op jit(solution)/shard_map/reduce_scatter | solution.py:42
  40.4 1.2 copy-start.2
  40.4 1.3 copy-start.1
  40.5 174.6 %all-gather.6.cloned.1.call-start = ((), (), s32[]{:S(2)}) async-start(), calls=%async_computation.4 | async-start | bytes 14579712 | tf_op jit(solution)/shard_map/all_gather | solution.py:36
  41.0 248.0 %all-gather.4.cloned.1.call-start = ((), (), s32[]{:S(2)}) async-start(), calls=%async_computation.2 | async-start | bytes 9216000 | tf_op jit(solution)/shard_map/all_gather | solution.py:34
Sparse Core Ops, SparseCore 0:
  40.5 169.9 reduce-scatter.1
Sparse Core Ops, SparseCore 1:
  42.8 73.7 all-gather.5
  118.0 171.0 all-gather.3
where the time goes:
time: 311 us; the launch traced here: 310 us
  waiting for transfers between devices  220 us (71%)
  local copies, waits for them, and re-layouts  20.7 us (7%)
  blocking collectives  19.6 us (6%)
  matrix products  18.1 us (6%)
  between operations  15.7 us (5%)
  other arithmetic  15.6 us (5%)
    reduce_scatter x1, waiting for transfers between devices, shards(): lax.psum_scatter(lax.dot_general(cycle_integrals, ordered, (((0,), (0,)),...  158 us
    all_gather x1, waiting for transfers between devices, shards(): integ_all = lax.all_gather(integrals, 'row', axis=0, tiled=True)  61.8 us
    all_to_all x1, blocking collectives, shards(): lax.all_to_all(regroup_in, ('col', 'depth'), split_axis=1, concat_axis=2,...  19.6 us
    dot_general x1, matrix products, shards(): jnp.dot(lax.all_gather(amplitudes, ('col', 'depth'), axis=1, tiled=True),...  13.9 us
    unnamed x7, local copies, waits for them, and re-layouts  12.2 us
    reduce_sum x4, other arithmetic, lookup(): return jnp.sum(jnp.where(matches, lookup_table[None, :], 0), axis=1)  10.9 us
  transfers between devices with their start and end apart: 3, of which 2 were waited for; matrix products, arithmetic and copies ran while one was open for 9% of the time, Pallas kernels for 0%

commit v1 on v0

--- a/solution.py
+++ b/solution.py
@@ -31,7 +31,12 @@
         .reshape(occ_block * CW, occ_here * NV)
     )
     columns = occ_here * NV
-    integ_all = lax.all_gather(integrals, "row", axis=0, tiled=True)
+    ring = [integrals]
+    for hop in range(3):
+        ring.append(lax.ppermute(ring[-1], "row", [(dev, (dev + 1) % 4) for dev in range(4)]))
+    integ_all = jnp.roll(
+        jnp.concatenate(ring[::-1], axis=0), (lax.axis_index("row") + 1) * ring[0].shape[0], axis=0
+    )
     ladder_sum = jnp.dot(
         lax.all_gather(amplitudes, ("col", "depth"), axis=1, tiled=True),
         integ_all,

time: 311 us -> 343 us (1.10)
  starting transfers between devices: 0.3 us -> 37.8 us
  waiting for transfers between devices: 220 us -> 195 us
  local copies, waits for them, and re-layouts: 20.7 us -> 41.6 us
    ppermute x0 -> x3, waiting for transfers between devices: none -> 194 us  [shards(): lax.ppermute(ring[-1], 'row', [(dev, (dev + 1) % 4) for dev in range(4)])]
    reduce_scatter x1, waiting for transfers between devices: 158 us -> 0.01 us  [shards(): lax.psum_scatter(lax.dot_general(cycle_integrals, ordered, (((0,), (0,)),...]
    all_gather x1 -> x0, waiting for transfers between devices: 61.8 us -> none  [shards(): integ_all = lax.all_gather(integrals, 'row', axis=0, tiled=True)]
    ppermute x0 -> x3, starting transfers between devices: none -> 37.7 us  [shards(): lax.ppermute(ring[-1], 'row', [(dev, (dev + 1) % 4) for dev in range(4)])]
    unnamed x7 -> x16, local copies, waits for them, and re-layouts: 12.2 us -> 31.7 us
  transfers between devices with their start and end apart: 3 -> 5, of which waited for: 2 -> 3; matrix products, arithmetic and copies ran while one was open for 9% -> 10% of each run, Pallas kernels for 0% -> 0%
where the time goes in v1:
time: 343 us
  waiting for transfers between devices  195 us (57%)
  local copies, waits for them, and re-layouts  41.6 us (12%)
  starting transfers between devices  37.8 us (11%)
  blocking collectives  19.6 us (6%)
  matrix products  18 us (5%)
  other arithmetic  15.6 us (5%)
  between operations  15.6 us (5%)
    ppermute x3, waiting for transfers between devices, shards(): lax.ppermute(ring[-1], 'row', [(dev, (dev + 1) % 4) for dev in range(4)])  194 us
    ppermute x3, starting transfers between devices, shards(): lax.ppermute(ring[-1], 'row', [(dev, (dev + 1) % 4) for dev in range(4)])  37.7 us
    unnamed x16, local copies, waits for them, and re-layouts  31.7 us
    all_to_all x1, blocking collectives, shards(): lax.all_to_all(regroup_in, ('col', 'depth'), split_axis=1, concat_axis=2,...  19.6 us
    dot_general x1, matrix products, shards(): jnp.dot(lax.all_gather(amplitudes, ('col', 'depth'), axis=1, tiled=True),...  13.9 us
    reduce_sum x4, other arithmetic, lookup(): return jnp.sum(jnp.where(matches, lookup_table[None, :], 0), axis=1)  10.9 us
  transfers between devices with their start and end apart: 5, of which 3 were waited for; matrix products, arithmetic and copies ran while one was open for 10% of the time, Pallas kernels for 0%

profile of v1, /device:TPU:0, one launch (start us, length us, event | category | flops | bytes accessed | tf_op | source)
XLA Modules:
  0.0 343.0 jit_solution(14730393984190240144)
XLA Ops:
  8.0 0.0 copy-start
  8.0 0.0 reduce-scatter.2.cloned.1.call-start
  8.1 3.8 %reshape.104 = bf16[8,100,900]{1,0,2:T(8,128)(2,1)S(1)} reshape(bf16[800,900]{0,1:T(8,128)(2,1)} %param.5) | data formatting | bytes 2880000 | tf_op jit(solution)/shard_map/reshape | solution.py:25
  11.8 2.8 copy.15
  14.7 19.6 %all_to_all.4 = bf16[8,64,900]{2,0,1:T(8,128)(2,1)S(1)} all-to-all(bf16[8,64,900]{2,0,1:T(8,128)(2,1)S(1)} %copy.15), channel_id=1, replica_groups=mesh['row'=4,'col'=2,'depth'=4] {'col','depth'}, dimensions={1} | all-to-all | bytes 1843200 | tf_op jit(solution)/shard_map/all_to_all | solution.py:26
  34.3 0.6 copy.16
  34.9 1.3 reshape.100
  36.2 0.0 copy-done
  36.2 4.2 %fusion.27 = f32[256,7200]{1,0:T(8,128)} fusion(bf16[64,256]{1,0:T(8,128)(2,1)S(1)} %copy-done, bf16[64,7200]{1,0:T(8,128)(2,1)S(1)} %reshape.100), kind=kOutput, calls=%fused_computation.103 | convolution fusion | flops 235929600 | bytes 8327168 | tf_op jit(solution)/shard_map/dot_general | solution.py:48
  40.4 0.0 copy-start.1
  40.4 0.0 copy-start.3
  40.4 0.0 copy-start.2
  40.4 0.0 reduce-scatter.2.cloned.1.call-update
  40.4 0.0 all-gather.3.cloned.1.call-start
  40.4 0.5 all-gather.3.cloned.1.call-update
  41.0 0.9 copy-done.1
  41.9 1.6 collective-permute-start
  43.4 78.3 %collective-permute-done = bf16[1800,512]{1,0:T(8,128)(2,1)} collective-permute-done((bf16[1800,512]{1,0:T(8,128)(2,1)S(1)}, bf16[1800,512]{1,0:T(8,128)(2,1)}, u32[]{:S(2)}, u32[]{:S(2)}) %collective-permute-start) | collective-permute-done | bytes 1843232 | tf_op jit(solution)/shard_map/ppermute | solution.py:36
  121.8 34.9 %collective-permute-start.1 = (bf16[1800,512]{1,0:T(8,128)(2,1)}, bf16[1800,512]{1,0:T(8,128)(2,1)}, u32[]{:S(2)}, u32[]{:S(2)}) collective-permute-start(bf16[1800,512]{1,0:T(8,128)(2,1)} %collective-permute-done), channel_id=1, source_target_pairs={{0,8},{8,16},{16,24},{24,0},{1,9},{9,17},{17,25},{25,1},{2,10},{10... | collective-permute-start | bytes 5529608 | tf_op jit(solution)/shard_map/ppermute | solution.py:36
  156.7 0.0 copy-done.3
  156.7 0.0 copy-done.2
  156.8 1.1 select_reduce_fusion.5
  157.9 80.1 %collective-permute-done.1 = bf16[1800,512]{1,0:T(8,128)(2,1)} collective-permute-done((bf16[1800,512]{1,0:T(8,128)(2,1)}, bf16[1800,512]{1,0:T(8,128)(2,1)}, u32[]{:S(2)}, u32[]{:S(2)}) %collective-permute-start.1) | collective-permute-done | bytes 1843232 | tf_op jit(solution)/shard_map/ppermute | solution.py:36
  238.0 1.2 collective-permute-start.2
  239.2 9.3 %select_reduce_fusion.2 = (s32[7200]{0:T(1024)S(1)}, s32[7200]{0:T(1024)S(1)}, s32[7200]{0:T(1024)S(1)}) fusion(s32[900]{0:T(1024)S(1)} %get-tuple-element.16, s32[7200]{0:T(1024)S(1)} %get-tuple-element.20, s32[900]{0:T(1024)S(1)} %get-tuple-element.15, s32[900]{0:T(1024)S(1)} %get-tuple-element.14), kind=kLoop, calls=%fused_computation.2 | loop fusion | flops 45338400 | bytes 126000 | tf_op jit(solution)/shard_map/reduce_sum | solution.py:18
  248.6 0.2 select_reduce_fusion.11
  248.8 0.3 select_reduce_fusion.8
  249.1 35.8 %collective-permute-done.2 = bf16[1800,512]{1,0:T(8,128)(2,1)} collective-permute-done((bf16[1800,512]{1,0:T(8,128)(2,1)}, bf16[1800,512]{1,0:T(8,128)(2,1)}, u32[]{:S(2)}, u32[]{:S(2)}) %collective-permute-start.2) | collective-permute-done | bytes 1843232 | tf_op jit(solution)/shard_map/ppermute | solution.py:36
  284.9 2.9 constant_dynamic-update-slice_fusion.7
  287.8 2.8 constant_dynamic-update-slice_fusion.6
  290.6 2.9 constant_dynamic-update-slice_fusion.5
  293.5 1.4 constant_dynamic-update-slice_fusion.4
  294.9 2.9 constant_dynamic-update-slice_fusion.3
  297.8 2.9 constant_dynamic-update-slice_fusion.2
  300.7 2.9 constant_dynamic-update-slice_fusion.1
  303.5 1.4 constant_dynamic-update-slice_fusion
  304.9 0.0 reduce-scatter.2.cloned.1.call-done
  304.9 4.6 %select_convert_fusion = bf16[64,7200]{1,0:T(8,128)(2,1)} fusion(f32[64,7200]{1,0:T(8,128)} %reduce-scatter.2.cloned.1.call-done, s32[7200]{0:T(1024)S(1)} %add.238, s32[64]{0:T(128)S(1)} %add.236, s32[7200]{0:T(1024)S(1)} %add.229, s32[64]{0:T(128)S(1)} %add.227, s32[7200]{0:T(1024)S(1)} %add.221, s32[64]{0:T(128)S(1)} %add.215), kind=kLoop, calls=%fused_computation.31 | loop fusion | flops 18432000 | bytes 2851968 | tf_op jit(solution)/shard_map/convert_element_type | solution.py:68
  309.5 0.0 all-gather.3.cloned.1.call-done
  309.5 12.2 %reshape.103 = bf16[7200,800]{1,0:T(8,128)(2,1)} reshape(bf16[8,900,800]{2,1,0:T(8,128)(2,1)} %all-gather.3.cloned.1.call-done) | data formatting | bytes 23040000
  321.6 13.9 %fusion.11 = bf16[800,512]{1,0:T(8,128)(2,1)} fusion(bf16[7200,800]{1,0:T(8,128)(2,1)} %reshape.103, bf16[14400,512]{1,0:T(8,128)(2,1)} %constant_dynamic-update-slice_fusion, s32[]{:T(128)S(6)} %select_n.154), kind=kOutput, calls=%fused_computation.33 | convolution fusion | flops 5898649600 | bytes 21094404 | tf_op jit(solution)/shard_map/dot_general | solution.py:40
  (10 shorter events, 0.1 us)
Async XLA Ops:
  8.0 28.2 %copy-start = (bf16[64,256]{1,0:T(8,128)(2,1)S(1)}, bf16[64,256]{1,0:T(8,128)(2,1)}, u32[]{:S(2)}) copy-start(bf16[64,256]{1,0:T(8,128)(2,1)} %param.7) | copy-start | bytes 98308
  8.0 296.9 %reduce-scatter.2.cloned.1.call-start = ((), (), s32[]{:S(2)}) async-start(), calls=%async_computation.2 | async-start | bytes 9338880 | tf_op jit(solution)/shard_map/reduce_scatter | solution.py:47
  40.4 1.5 copy-start.1
  40.4 116.3 %copy-start.3 = (s32[100]{0:T(128)S(1)}, s32[100]{0:T(128)}, u32[]{:S(2)}) copy-start(s32[100]{0:T(128)} %param.8) | copy-start | bytes 1204
  40.4 116.4 %copy-start.2 = (s32[900]{0:T(1024)S(1)}, s32[900]{0:T(1024)}, u32[]{:S(2)}) copy-start(s32[900]{0:T(1024)} %param.9) | copy-start | bytes 10804
  40.4 269.1 %all-gather.3.cloned.1.call-start = ((), (), s32[]{:S(2)}) async-start(), calls=%async_computation.3 | async-start | bytes 14579712 | tf_op jit(solution)/shard_map/all_gather | solution.py:41
  41.9 79.9 %collective-permute-start = (bf16[1800,512]{1,0:T(8,128)(2,1)S(1)}, bf16[1800,512]{1,0:T(8,128)(2,1)}, u32[]{:S(2)}, u32[]{:S(2)}) collective-permute-start(bf16[1800,512]{1,0:T(8,128)(2,1)S(1)} %copy-done.1), channel_id=1, source_target_pairs={{0,8},{8,16},{16,24},{24,0},{1,9},{9,17},{17,25},{25,1},{2,10},{10... | collective-permute-start | bytes 5529608 | tf_op jit(solution)/shard_map/ppermute | solution.py:36
  121.8 116.2 %collective-permute-start.1 = (bf16[1800,512]{1,0:T(8,128)(2,1)}, bf16[1800,512]{1,0:T(8,128)(2,1)}, u32[]{:S(2)}, u32[]{:S(2)}) collective-permute-start(bf16[1800,512]{1,0:T(8,128)(2,1)} %collective-permute-done), channel_id=1, source_target_pairs={{0,8},{8,16},{16,24},{24,0},{1,9},{9,17},{17,25},{25,1},{2,10},{10... | collective-permute-start | bytes 5529608 | tf_op jit(solution)/shard_map/ppermute | solution.py:36
  238.0 46.9 %collective-permute-start.2 = (bf16[1800,512]{1,0:T(8,128)(2,1)}, bf16[1800,512]{1,0:T(8,128)(2,1)}, u32[]{:S(2)}, u32[]{:S(2)}) collective-permute-start(bf16[1800,512]{1,0:T(8,128)(2,1)} %collective-permute-done.1), channel_id=1, source_target_pairs={{0,8},{8,16},{16,24},{24,0},{1,9},{9,17},{17,25},{25,1},{2,10},{10... | collective-permute-start | bytes 5529608 | tf_op jit(solution)/shard_map/ppermute | solution.py:36
Sparse Core Ops, SparseCore 0:
  40.5 209.2 reduce-scatter.1
Sparse Core Ops, SparseCore 1:
  42.8 73.7 all-gather.2
